TPU v7x, 32 devices: a whole 2x2x4 slice. The times are simulated.
32 devices in a mesh: group: 2 (over y), visit: 16 (over z, x, core), sky: 1.
Axes of the slice: x: 2, y: 2, z: 4, core: 2. Of those that a mesh axis runs over, the one named last changes fastest.
Arguments:
- template: bfloat16 [64, 128], P(('group', 'visit'), 'sky'), parts along dimension 0, may hold values from -6 to 6
- science: float32 [32, 32, 128], P(('group', 'visit'), None, 'sky'), parts along dimension 0, may hold values from -15 to 15
- variance: float32 [32, 32, 128], P(('group', 'visit'), None, 'sky'), parts along dimension 0, may hold values from 0.5 to 4
- col_taps: bfloat16 [49, 31], replicated, may hold values from -1 to 1
- row_taps: bfloat16 [49, 31], replicated, may hold values from -1 to 1
- stamp_rows: int32 [32, 1, 16], P(('group', 'visit'), 'sky'), parts along dimension 0, may hold values from 0 to 16
- stamp_cols: int32 [32, 1, 16], P(('group', 'visit'), 'sky'), parts along dimension 0, may hold values from 0 to 112
Outputs:
- difference: float32 [32, 32, 128], P(('group', 'visit'), None, 'sky'), parts along dimension 0
- coefficients: float32 [32, 50], P(('group', 'visit')), parts along dimension 0
- detection: float32 [64, 128], P(('group', 'visit'), 'sky'), parts along dimension 0
There are 2 independent parts, one for each index of `group`. A program takes and returns all parts, laid end to end along the dimension named above; an argument that names none is the same for every part. Nothing has to cross between parts.
All inputs are finite; a program needn't handle non-finite values.
Results may differ from a plain program's by a relative error of at most 0.0018.
Values may be sent and summed in bfloat16 or wider, within the bound.
No kernel may reach another device: no remote copies, remote signals or barrier semaphores. Data moves between devices by JAX's collectives and lax.ppermute only.
A program may use at most 128 MiB of HBM per device.

v0:
```python
import jax
import jax.numpy as jnp
from jax import lax
from jax.sharding import PartitionSpec as P

KBLK = 7
STAMP = 16


def with_halo(cells, sides, width):
    for axis, dim in sides:
        count = lax.axis_size(axis)
        ends = count - 1
        head = lax.slice_in_dim(cells, 0, width, axis=dim)
        tail = lax.slice_in_dim(cells, cells.shape[dim] - width, cells.shape[dim], axis=dim)
        cells = jnp.concatenate(
            [
                lax.ppermute(tail, axis, [(i, (i + 1) % count) for i in range(ends)]),
                cells,
                lax.ppermute(head, axis, [((i + 1) % count, i) for i in range(ends)]),
            ],
            axis=dim,
        )
    return cells


def tap_selectors(out_len, in_len, tap_count):
    offsets = (
        jnp.arange(in_len, dtype=jnp.int32)[None, :] - jnp.arange(out_len, dtype=jnp.int32)[:, None]
    )
    return (offsets[None, :, :] == jnp.arange(tap_count, dtype=jnp.int32)[:, None, None]).astype(
        jnp.float32
    )


def column_pass(padded, taps_block):
    tap_count = taps_block.shape[1]
    out_width = padded.shape[1] - tap_count + 1
    selectors = tap_selectors(out_width, padded.shape[1], tap_count)
    band_mats = jnp.einsum("kj,jci->kic", taps_block.astype(jnp.float32), selectors).astype(
        jnp.bfloat16
    )
    result = jnp.einsum("ri,kic->krc", padded, band_mats, preferred_element_type=jnp.float32)
    return result.astype(jnp.bfloat16)


def band_matrix(taps_block, out_len, in_len):
    tap_count = taps_block.shape[1]
    offsets = (
        jnp.arange(in_len, dtype=jnp.int32)[None, :] - jnp.arange(out_len, dtype=jnp.int32)[:, None]
    )
    taps_wide = taps_block.astype(jnp.float32)
    band = jnp.zeros((taps_block.shape[0], out_len, in_len), jnp.float32)
    for offset in range(tap_count):
        band = band + jnp.where(
            offsets[None, :, :] == offset, taps_wide[:, offset][:, None, None], 0.0
        )
    return band.astype(jnp.bfloat16)


def row_pass(columns, taps_block):
    tap_count = taps_block.shape[1]
    margin = (tap_count - 1) // 2
    height = columns.shape[1]
    stride = min(512, height)
    padded = jnp.pad(columns, ((0, 0), (margin, margin), (0, 0)))
    band = band_matrix(taps_block, stride, stride + 2 * margin)
    pieces = jnp.einsum("kti,kiw->ktw", band, padded, preferred_element_type=jnp.float32).astype(
        jnp.bfloat16
    )
    return pieces


def extract_stamps(block, row_starts, col_starts):

    def extract(row_start, col_start):
        return lax.dynamic_slice(
            block, (jnp.int32(0), row_start, col_start), (block.shape[0], STAMP, STAMP)
        )

    stamps = jax.vmap(extract)(row_starts, col_starts)
    return jnp.transpose(stamps, (1, 0, 2, 3)).reshape(block.shape[0], -1)


def extract_plane(plane, row_starts, col_starts):

    def extract(row_start, col_start):
        return lax.dynamic_slice(plane, (row_start, col_start), (STAMP, STAMP))

    return jax.vmap(extract)(row_starts, col_starts).reshape(-1)


def cholesky_solve(matrix, vector):
    factor = jnp.linalg.cholesky(matrix)
    middle = lax.linalg.triangular_solve(factor, vector[:, None], left_side=True, lower=True)
    answer = lax.linalg.triangular_solve(
        factor, middle, left_side=True, lower=True, transpose_a=True
    )
    return answer[:, 0]


def on_device(template, science, variance, col_taps, row_taps, stamp_rows, stamp_cols):
    tap_count = col_taps.shape[1]
    margin = (tap_count - 1) // 2
    kernels = col_taps.shape[0]
    blocks = kernels // KBLK
    science_map = science[0]
    variance_map = variance[0]
    inverse = 1.0 / variance_map
    gathered = lax.all_gather(template, "visit", axis=0, tiled=True)
    padded_tile = with_halo(gathered, (("sky", 1),), margin)
    image_list = []
    for block_index in range(blocks):
        image_list.append(
            row_pass(
                column_pass(padded_tile, col_taps[block_index * KBLK : (block_index + 1) * KBLK]),
                row_taps[block_index * KBLK : (block_index + 1) * KBLK],
            )
        )
    convolved = jnp.concatenate(image_list, axis=0)
    row_starts = stamp_rows[0, 0]
    col_starts = stamp_cols[0, 0]
    design_core = extract_stamps(convolved, row_starts, col_starts)
    design = jnp.concatenate(
        [design_core, jnp.ones((1, design_core.shape[1]), design_core.dtype)], axis=0
    ).astype(jnp.float32)
    weights = 1.0 / extract_plane(variance_map, row_starts, col_starts)
    values = extract_plane(science_map, row_starts, col_starts)
    partial_normal = jnp.dot(design * weights[None, :], design.T, precision=lax.Precision.HIGHEST)
    partial_target = jnp.dot(design, weights * values, precision=lax.Precision.HIGHEST)
    normal, target = lax.psum((partial_normal, partial_target), "sky")
    solution = cholesky_solve(normal, target)

    def model_step(block_index, total):
        images = lax.dynamic_slice_in_dim(convolved, block_index * KBLK, KBLK, 0).astype(
            jnp.float32
        )
        share = lax.dynamic_slice_in_dim(solution, block_index * KBLK, KBLK, 0)
        return total + jnp.tensordot(share, images, axes=1, precision=lax.Precision.HIGHEST)

    model_map = lax.fori_loop(0, blocks, model_step, jnp.zeros(science_map.shape, jnp.float32))
    residual = science_map - model_map - solution[kernels]
    difference = (residual / jnp.sqrt(variance_map))[None, :, :]
    weighted = residual / variance_map
    numerator, weight_total = (
        lax.psum_scatter(weighted, "visit", scatter_dimension=0, tiled=True),
        lax.psum_scatter(inverse, "visit", scatter_dimension=0, tiled=True),
    )
    detection = numerator / jnp.sqrt(weight_total)
    return (difference, solution[None, :], detection)


def solution(mesh):
    in_specs = (
        P(("group", "visit"), "sky"),
        P(("group", "visit"), None, "sky"),
        P(("group", "visit"), None, "sky"),
        P(),
        P(),
        P(("group", "visit"), "sky", None),
        P(("group", "visit"), "sky", None),
    )
    out_specs = (
        P(("group", "visit"), None, "sky"),
        P(("group", "visit"), None),
        P(("group", "visit"), "sky"),
    )
    return jax.shard_map(
        on_device, mesh=mesh, in_specs=in_specs, out_specs=out_specs, check_vma=False
    )
```

profile of v0, /device:TPU:0, one launch (start us, length us, event | category | flops | bytes accessed | tf_op | source)
XLA Modules:
  0.0 237.8 jit_solution(4948356048800179354)
XLA Ops:
  0.6 23.3 %all-gather = bf16[16,2,128]{2,1,0:T(2,128)(2,1)S(1)} all-gather(bf16[1,2,128]{2,1,0:T(2,128)(2,1)} %bitcast.593), channel_id=1, replica_groups=mesh['group'=2,'visit'=16,'sky'=1] {'visit'}, dimensions={0}, use_global_device_ids=true | all-gather | bytes 8704 | tf_op jit(solution)/shard_map/all_gather | solution.py:110
  26.7 1.7 fusion.34
  28.4 1.8 fusion.33
  30.2 1.7 fusion.32
  32.0 1.8 fusion.31
  33.9 1.8 fusion.30
  35.7 1.8 fusion.29
  37.6 1.9 fusion.28
  39.5 30.6 %while.18 = (s32[]{:T(128)}, f32[32,128]{1,0:T(8,128)S(1)}, s32[16,2]{0,1:T(2,128)S(1)}, f32[16,16,16]{2,1,0:T(8,128)S(1)}, s32[]{:T(128)}) while((s32[]{:T(128)}, f32[32,128]{1,0:T(8,128)S(1)}, s32[16,2]{0,1:T(2,128)S(1)}, f32[16,16,16]{2,1,0:T(8,128)S(1)}, s32[]{:T(128)}) %tuple.319), condition=%wide.while_cond.1, body=%wide.while_body.1.sunk | while | flops 2 | bytes 16493 | solution.py:88
  40.3 1.3 bitcast_dynamic-update-slice_fusion.7
  42.2 1.3 bitcast_dynamic-update-slice_fusion.7
  44.1 1.3 bitcast_dynamic-update-slice_fusion.7
  46.0 1.3 bitcast_dynamic-update-slice_fusion.7
  47.9 1.3 bitcast_dynamic-update-slice_fusion.7
  49.8 1.3 bitcast_dynamic-update-slice_fusion.7
  51.7 1.3 bitcast_dynamic-update-slice_fusion.7
  53.6 1.3 bitcast_dynamic-update-slice_fusion.7
  55.5 1.3 bitcast_dynamic-update-slice_fusion.7
  57.4 1.3 bitcast_dynamic-update-slice_fusion.7
  59.3 1.3 bitcast_dynamic-update-slice_fusion.7
  61.2 1.3 bitcast_dynamic-update-slice_fusion.7
  63.1 1.3 bitcast_dynamic-update-slice_fusion.7
  65.0 1.3 bitcast_dynamic-update-slice_fusion.7
  66.9 1.3 bitcast_dynamic-update-slice_fusion.7
  70.1 31.5 %while.19 = (s32[]{:T(128)}, f32[32,128]{1,0:T(8,128)S(1)}, s32[16,2]{0,1:T(2,128)S(1)}, f32[16,16,16]{2,1,0:T(8,128)S(1)}, s32[]{:T(128)}) while((s32[]{:T(128)}, f32[32,128]{1,0:T(8,128)S(1)}, s32[16,2]{0,1:T(2,128)S(1)}, f32[16,16,16]{2,1,0:T(8,128)S(1)}, s32[]{:T(128)}) %tuple.321), condition=%wide.while_cond.2, body=%wide.while_body.2.sunk | while | flops 2 | bytes 16493 | solution.py:88
  70.7 1.4 bitcast_dynamic-update-slice_fusion.8
  72.7 1.4 bitcast_dynamic-update-slice_fusion.8
  74.7 1.4 bitcast_dynamic-update-slice_fusion.8
  76.6 1.4 bitcast_dynamic-update-slice_fusion.8
  78.6 1.4 bitcast_dynamic-update-slice_fusion.8
  80.6 1.4 bitcast_dynamic-update-slice_fusion.8
  82.5 1.4 bitcast_dynamic-update-slice_fusion.8
  84.5 1.4 bitcast_dynamic-update-slice_fusion.8
  86.5 1.4 bitcast_dynamic-update-slice_fusion.8
  88.4 1.4 bitcast_dynamic-update-slice_fusion.8
  90.4 1.4 bitcast_dynamic-update-slice_fusion.8
  92.4 1.4 bitcast_dynamic-update-slice_fusion.8
  94.3 1.4 bitcast_dynamic-update-slice_fusion.8
  96.3 1.4 bitcast_dynamic-update-slice_fusion.8
  98.3 1.4 bitcast_dynamic-update-slice_fusion.8
  100.2 1.4 bitcast_dynamic-update-slice_fusion.8
  112.6 45.1 %while.17 = (s32[]{:T(128)}, bf16[49,32,128]{2,1,0:T(8,128)(2,1)S(1)}, s32[16,3]{0,1:T(4,128)S(1)}, bf16[16,49,16,16]{3,2,1,0:T(8,128)(2,1)}, s32[]{:T(128)}) while((s32[]{:T(128)}, bf16[49,32,128]{2,1,0:T(8,128)(2,1)S(1)}, s32[16,3]{0,1:T(4,128)S(1)}, bf16[16,49,16,16]{3,2,1,0:T(8,128)(2,1)}, s32[]{:T(128)}) %tuple.312), condition=%wide.while_cond, body=%wide.while_body.sunk | while | flops 2 | bytes 227433 | solution.py:77
  113.3 2.1 bitcast_dynamic-update-slice_fusion.6
  116.1 2.1 bitcast_dynamic-update-slice_fusion.6
  118.9 2.2 bitcast_dynamic-update-slice_fusion.6
  121.8 2.2 bitcast_dynamic-update-slice_fusion.6
  124.6 2.1 bitcast_dynamic-update-slice_fusion.6
  127.4 2.2 bitcast_dynamic-update-slice_fusion.6
  130.2 2.1 bitcast_dynamic-update-slice_fusion.6
  133.0 2.2 bitcast_dynamic-update-slice_fusion.6
  135.9 2.1 bitcast_dynamic-update-slice_fusion.6
  138.7 2.2 bitcast_dynamic-update-slice_fusion.6
  141.5 2.2 bitcast_dynamic-update-slice_fusion.6
  144.3 2.2 bitcast_dynamic-update-slice_fusion.6
  147.1 2.2 bitcast_dynamic-update-slice_fusion.6
  150.0 2.1 bitcast_dynamic-update-slice_fusion.6
  152.8 2.2 bitcast_dynamic-update-slice_fusion.6
  155.6 2.1 bitcast_dynamic-update-slice_fusion.6
  157.7 4.3 %copy.27 = bf16[49,16,16,16]{0,3,2,1:T(8,128)(2,1)S(1)} copy(bf16[49,16,16,16]{3,2,0,1:T(8,128)(2,1)} %bitcast.581) | data formatting | bytes 802816 | tf_op jit(solution)/shard_map/transpose | solution.py:82
  162.1 2.4 %fusion.11 = f32[50,50]{1,0:T(8,128)S(1)} fusion(f32[4096]{0:T(1024)S(1)} %div.38, bf16[49,4096]{0,1:T(8,128)(2,1)S(1)} %bitcast.579), kind=kOutput, calls=%fused_computation.20 | convolution fusion | flops 123289600 | bytes 427792 | tf_op jit(solution)/shard_map/dot_general | solution.py:129
  164.6 4.6 %cholesky.16 = f32[50,50]{1,0:T(8,128)S(1)} custom-call(f32[50,50]{1,0:T(8,128)S(1)} %fusion.511), custom_call_target="Cholesky" | custom-call | tf_op jit(solution)/shard_map/jit(cholesky)/cholesky | solution.py:94
  170.5 3.8 %custom-call.8 = f32[1,50,50]{1,2,0:T(8,128)S(1)} custom-call(f32[1,50,50]{2,1,0:T(8,128)S(1)} %fusion.507), custom_call_target="InvertDiagBlocksLowerTriangular" | custom-call | tf_op jit(solution)/shard_map/triangular_solve | solution.py:96
  175.8 2.3 while.20
  179.5 57.8 %all-reduce.10 = (f32[32,128]{1,0:T(8,128)S(1)}, f32[32,128]{1,0:T(8,128)S(1)}) all-reduce(f32[32,128]{1,0:T(8,128)S(1)} %get-tuple-element.164, f32[32,128]{1,0:T(8,128)S(1)} %get-tuple-element.162), channel_id=3, replica_groups=mesh['group'=2,'visit'=16,'sky'=1] {'visit'}, use_global_device_ids=true, to_apply=%region_5.6.clone | all-reduce | flops 8192 | bytes 65536
  (210 shorter events, 50.6 us)
Async XLA Ops:
  0.6 31.4 %copy-start.5 = (bf16[49,31]{0,1:T(8,128)(2,1)S(1)}, bf16[49,31]{0,1:T(8,128)(2,1)}, u32[]{:S(2)}) copy-start(bf16[49,31]{0,1:T(8,128)(2,1)} %param.12) | copy-start | bytes 9118
  24.0 79.1 %collective-permute-start = (bf16[32,15]{1,0:T(8,128)(2,1)S(1)}, bf16[32,15]{1,0:T(8,128)(2,1)S(1)}, u32[]{:S(2)}, u32[]{:S(2)}) collective-permute-start(bf16[32,15]{1,0:T(8,128)(2,1)S(1)} %get-tuple-element.389), channel_id=1, source_target_pairs={} | collective-permute-start | bytes 2888 | tf_op jit(solution)/shard_map/ppermute | solution.py:18
  24.6 78.5 %collective-permute-start.1 = (bf16[32,15]{1,0:T(8,128)(2,1)S(1)}, bf16[32,15]{1,0:T(8,128)(2,1)S(1)}, u32[]{:S(2)}, u32[]{:S(2)}) collective-permute-start(bf16[32,15]{1,0:T(8,128)(2,1)S(1)} %get-tuple-element.390), channel_id=1, source_target_pairs={} | collective-permute-start | bytes 2888 | tf_op jit(solution)/shard_map/ppermute | solution.py:20
  28.4 11.0 %copy-start.3 = (s32[1,1,16]{2,1,0:T(1,128)S(1)}, s32[1,1,16]{2,1,0:T(1,128)}, u32[]{:S(2)}) copy-start(s32[1,1,16]{2,1,0:T(1,128)} %param.15) | copy-start | bytes 196
  28.4 11.0 %copy-start.4 = (s32[1,1,16]{2,1,0:T(1,128)S(1)}, s32[1,1,16]{2,1,0:T(1,128)}, u32[]{:S(2)}) copy-start(s32[1,1,16]{2,1,0:T(1,128)} %param.14) | copy-start | bytes 196
  30.2 9.3 %copy-start = (f32[1,32,128]{2,1,0:T(8,128)S(1)}, f32[1,32,128]{2,1,0:T(8,128)}, u32[]{:S(2)}) copy-start(f32[1,32,128]{2,1,0:T(8,128)} %param.11) | copy-start | bytes 49156
  30.2 39.9 %copy-start.1 = (f32[1,32,128]{2,1,0:T(8,128)S(1)}, f32[1,32,128]{2,1,0:T(8,128)}, u32[]{:S(2)}) copy-start(f32[1,32,128]{2,1,0:T(8,128)} %param.10) | copy-start | bytes 49156
  32.0 69.9 %copy-start.6 = (u32[32]{0:T(128)S(1)}, u32[32]{0:T(128)}, u32[]{:S(2)}) copy-start(u32[32]{0:T(128)} %constant.223) | copy-start | bytes 388
  103.1 4.8 %copy-start.7 = (bf16[7,158,128]{1,0,2:T(8,128)(2,1)S(1)}, bf16[7,158,128]{1,0,2:T(8,128)(2,1)}, u32[]{:S(2)}) copy-start(bf16[7,158,128]{1,0,2:T(8,128)(2,1)} %fusion.28) | copy-start | bytes 849412
  178.2 59.7 %copy-start.2 = (f32[50]{0:T(128)}, f32[50]{0:T(128)S(1)}, u32[]{:S(2)}) copy-start(f32[50]{0:T(128)S(1)} %get-tuple-element.611) | copy-start | bytes 604
where the time goes:
time: 239 us; the launch traced here: 238 us
  local copies, waits for them, and re-layouts  113 us (47%)
  blocking collectives  81.1 us (34%)
  matrix products  27 us (11%)
  other arithmetic  13 us (5%)
    gather x144, local copies, waits for them, and re-layouts  107 us
    unnamed x1, blocking collectives  57.8 us
    all_gather x1, blocking collectives, on_device(): gathered = lax.all_gather(template, 'visit', axis=0, tiled=True)  23.3 us
    dot_general x7, matrix products, column_pass(): jnp.einsum('kj,jci->kic', taps_block.astype(jnp.float32), selectors)  12.6 us
    another operation x3, other arithmetic, cholesky_solve(): factor = jnp.linalg.cholesky(matrix)  5.24 us
    dot_general x7, matrix products, column_pass(): jnp.einsum('ri,kic->krc', padded, band_mats, preferred_element_type=jnp.f...  4.89 us
  transfers between devices with their start and end apart: 2, of which 0 were waited for; matrix products, arithmetic and copies ran while one was open for 32% of the time, Pallas kernels for 0%

commit v1 on v0

--- a/solution.py
+++ b/solution.py
@@ -107,7 +107,16 @@
     science_map = science[0]
     variance_map = variance[0]
     inverse = 1.0 / variance_map
-    gathered = lax.all_gather(template, "visit", axis=0, tiled=True)
+    f_next, seen_now = (lax.axis_size("visit"), lax.axis_index("visit"))
+    gathered, piece_out = (template, 1)
+    while piece_out < f_next:
+        frame_out = lax.ppermute(
+            gathered, axis_name="visit", perm=[(b, b ^ piece_out) for b in range(f_next)]
+        )
+        u1 = jnp.concatenate([gathered, frame_out], 0)
+        res = jnp.concatenate([frame_out, gathered], 0)
+        gathered = jnp.where(seen_now & piece_out == 0, u1, res)
+        piece_out = 2 * piece_out
     padded_tile = with_halo(gathered, (("sky", 1),), margin)
     image_list = []
     for block_index in range(blocks):

time: 239 us -> 229 us (0.958)
  blocking collectives: 81.1 us -> 59 us
  starting transfers between devices: 1.3 us -> 9.8 us
  waiting for transfers between devices: 0.01 us -> 4.67 us
    all_gather x1 -> x0, blocking collectives: 23.3 us -> none  [on_device(): gathered = lax.all_gather(template, 'visit', axis=0, tiled=True)]
    ppermute x0 -> x4, starting transfers between devices: none -> 8.32 us  [on_device(): lax.ppermute(gathered, axis_name='visit', perm=[(b, b ^ piece_out) for b...]
    ppermute x0 -> x4, waiting for transfers between devices: none -> 4.66 us  [on_device(): lax.ppermute(gathered, axis_name='visit', perm=[(b, b ^ piece_out) for b...]
  transfers between devices with their start and end apart: 2 -> 6, of which waited for: 0 -> 3; matrix products, arithmetic and copies ran while one was open for 32% -> 34% of each run, Pallas kernels for 0% -> 0%
where the time goes in v1:
time: 229 us; the launch traced here: 227 us
  local copies, waits for them, and re-layouts  112 us (49%)
  blocking collectives  59 us (26%)
  matrix products  27 us (12%)
  other arithmetic  13 us (6%)
  starting transfers between devices  9.8 us (4%)
  waiting for transfers between devices  4.67 us (2%)
    gather x144, local copies, waits for them, and re-layouts  106 us
    unnamed x1, blocking collectives  59 us
    dot_general x7, matrix products, column_pass(): jnp.einsum('kj,jci->kic', taps_block.astype(jnp.float32), selectors)  12.5 us
    ppermute x4, starting transfers between devices, on_device(): lax.ppermute(gathered, axis_name='visit', perm=[(b, b ^ piece_out) for b...  8.32 us
    another operation x3, other arithmetic, cholesky_solve(): factor = jnp.linalg.cholesky(matrix)  5.24 us
    dot_general x7, matrix products, column_pass(): jnp.einsum('ri,kic->krc', padded, band_mats, preferred_element_type=jnp.f...  4.89 us
    ppermute x4, waiting for transfers between devices, on_device(): lax.ppermute(gathered, axis_name='visit', perm=[(b, b ^ piece_out) for b...  4.66 us
  transfers between devices with their start and end apart: 6, of which 3 were waited for; matrix products, arithmetic and copies ran while one was open for 34% of the time, Pallas kernels for 0%

profile of v1, /device:TPU:0, one launch (start us, length us, event | category | flops | bytes accessed | tf_op | source)
XLA Modules:
  0.0 227.5 jit_solution(17007917748574673735)
XLA Ops:
  2.5 1.7 fusion.34
  4.2 1.8 fusion.33
  6.0 1.7 fusion.32
  7.8 1.8 fusion.31
  9.7 1.8 fusion.30
  11.5 1.8 fusion.29
  13.4 1.9 fusion.28
  15.4 32.2 %while.18 = (s32[]{:T(128)}, f32[32,128]{1,0:T(8,128)S(1)}, s32[16,2]{0,1:T(2,128)S(1)}, f32[16,16,16]{2,1,0:T(8,128)S(1)}, s32[]{:T(128)}) while((s32[]{:T(128)}, f32[32,128]{1,0:T(8,128)S(1)}, s32[16,2]{0,1:T(2,128)S(1)}, f32[16,16,16]{2,1,0:T(8,128)S(1)}, s32[]{:T(128)}) %tuple.319), condition=%wide.while_cond.1, body=%wide.while_body.1.sunk | while | flops 2 | bytes 16493 | solution.py:88
  16.0 1.4 bitcast_dynamic-update-slice_fusion.7
  18.0 1.4 bitcast_dynamic-update-slice_fusion.7
  22.1 1.4 bitcast_dynamic-update-slice_fusion.7
  24.1 1.4 bitcast_dynamic-update-slice_fusion.7
  26.1 1.4 bitcast_dynamic-update-slice_fusion.7
  28.1 1.4 bitcast_dynamic-update-slice_fusion.7
  30.1 1.4 bitcast_dynamic-update-slice_fusion.7
  32.1 1.4 bitcast_dynamic-update-slice_fusion.7
  34.1 1.4 bitcast_dynamic-update-slice_fusion.7
  38.1 1.4 bitcast_dynamic-update-slice_fusion.7
  47.6 31.5 %while.19 = (s32[]{:T(128)}, f32[32,128]{1,0:T(8,128)S(1)}, s32[16,2]{0,1:T(2,128)S(1)}, f32[16,16,16]{2,1,0:T(8,128)S(1)}, s32[]{:T(128)}) while((s32[]{:T(128)}, f32[32,128]{1,0:T(8,128)S(1)}, s32[16,2]{0,1:T(2,128)S(1)}, f32[16,16,16]{2,1,0:T(8,128)S(1)}, s32[]{:T(128)}) %tuple.321), condition=%wide.while_cond.2, body=%wide.while_body.2.sunk | while | flops 2 | bytes 16493 | solution.py:88
  48.2 1.4 bitcast_dynamic-update-slice_fusion.8
  50.1 1.4 bitcast_dynamic-update-slice_fusion.8
  52.1 1.4 bitcast_dynamic-update-slice_fusion.8
  54.1 1.4 bitcast_dynamic-update-slice_fusion.8
  56.0 1.4 bitcast_dynamic-update-slice_fusion.8
  58.0 1.4 bitcast_dynamic-update-slice_fusion.8
  60.0 1.4 bitcast_dynamic-update-slice_fusion.8
  61.9 1.4 bitcast_dynamic-update-slice_fusion.8
  63.9 1.4 bitcast_dynamic-update-slice_fusion.8
  65.9 1.4 bitcast_dynamic-update-slice_fusion.8
  67.8 1.4 bitcast_dynamic-update-slice_fusion.8
  69.8 1.4 bitcast_dynamic-update-slice_fusion.8
  71.8 1.4 bitcast_dynamic-update-slice_fusion.8
  73.7 1.4 bitcast_dynamic-update-slice_fusion.8
  75.7 1.4 bitcast_dynamic-update-slice_fusion.8
  77.7 1.4 bitcast_dynamic-update-slice_fusion.8
  79.1 2.6 %collective-permute-start.1 = (bf16[4,128]{1,0:T(4,128)(2,1)S(1)}, bf16[4,128]{1,0:T(4,128)(2,1)S(1)}, u32[]{:S(2)}, u32[]{:S(2)}) collective-permute-start(bf16[4,128]{1,0:T(4,128)(2,1)S(1)} %maximum_select_fusion.3), channel_id=1, source_target_pairs={{0,2},{1,3},{2,0},{3,1},{4,6},{5,7},{6,4},{7,5},{8,10},{9,11},{10,... | collective-permute-start | bytes 3080 | tf_op jit(solution)/shard_map/ppermute | solution.py:113
  81.7 1.5 collective-permute-done.1
  83.2 2.2 collective-permute-start.2
  85.4 1.6 collective-permute-done.2
  87.0 3.0 %collective-permute-start.3 = (bf16[16,128]{1,0:T(8,128)(2,1)S(1)}, bf16[16,128]{1,0:T(8,128)(2,1)S(1)}, u32[]{:S(2)}, u32[]{:S(2)}) collective-permute-start(bf16[16,128]{1,0:T(8,128)(2,1)S(1)} %maximum_select_fusion.1), channel_id=1, source_target_pairs={{0,8},{1,9},{2,10},{3,11},{4,12},{5,13},{6,14},{7,15},{8,0},{9,1},... | collective-permute-start | bytes 12296 | tf_op jit(solution)/shard_map/ppermute | solution.py:113
  90.0 1.6 collective-permute-done.3
  104.2 42.0 %while.17 = (s32[]{:T(128)}, bf16[49,32,128]{2,1,0:T(8,128)(2,1)S(1)}, s32[16,3]{0,1:T(4,128)S(1)}, bf16[16,49,16,16]{3,2,1,0:T(8,128)(2,1)}, s32[]{:T(128)}) while((s32[]{:T(128)}, bf16[49,32,128]{2,1,0:T(8,128)(2,1)S(1)}, s32[16,3]{0,1:T(4,128)S(1)}, bf16[16,49,16,16]{3,2,1,0:T(8,128)(2,1)}, s32[]{:T(128)}) %tuple.312), condition=%wide.while_cond, body=%wide.while_body.sunk | while | flops 2 | bytes 227433 | solution.py:77
  104.8 2.0 bitcast_dynamic-update-slice_fusion.6
  107.4 2.0 bitcast_dynamic-update-slice_fusion.6
  110.0 2.0 bitcast_dynamic-update-slice_fusion.6
  112.6 2.1 bitcast_dynamic-update-slice_fusion.6
  115.3 2.0 bitcast_dynamic-update-slice_fusion.6
  117.9 2.0 bitcast_dynamic-update-slice_fusion.6
  120.6 2.0 bitcast_dynamic-update-slice_fusion.6
  123.2 2.0 bitcast_dynamic-update-slice_fusion.6
  125.8 2.0 bitcast_dynamic-update-slice_fusion.6
  128.4 2.0 bitcast_dynamic-update-slice_fusion.6
  131.0 2.0 bitcast_dynamic-update-slice_fusion.6
  133.7 2.0 bitcast_dynamic-update-slice_fusion.6
  136.3 2.0 bitcast_dynamic-update-slice_fusion.6
  138.9 2.0 bitcast_dynamic-update-slice_fusion.6
  141.5 2.0 bitcast_dynamic-update-slice_fusion.6
  144.2 2.0 bitcast_dynamic-update-slice_fusion.6
  146.2 4.3 %copy.27 = bf16[49,16,16,16]{0,3,2,1:T(8,128)(2,1)S(1)} copy(bf16[49,16,16,16]{3,2,0,1:T(8,128)(2,1)} %bitcast.579) | data formatting | bytes 802816 | tf_op jit(solution)/shard_map/transpose | solution.py:82
  150.5 2.4 %fusion.11 = f32[50,50]{1,0:T(8,128)S(1)} fusion(f32[4096]{0:T(1024)S(1)} %div.38, bf16[49,4096]{0,1:T(8,128)(2,1)S(1)} %bitcast.577), kind=kOutput, calls=%fused_computation.20 | convolution fusion | flops 123289600 | bytes 427792 | tf_op jit(solution)/shard_map/dot_general | solution.py:138
  153.1 4.6 %cholesky.16 = f32[50,50]{1,0:T(8,128)S(1)} custom-call(f32[50,50]{1,0:T(8,128)S(1)} %fusion.511), custom_call_target="Cholesky" | custom-call | tf_op jit(solution)/shard_map/jit(cholesky)/cholesky | solution.py:94
  159.0 3.8 %custom-call.8 = f32[1,50,50]{1,2,0:T(8,128)S(1)} custom-call(f32[1,50,50]{2,1,0:T(8,128)S(1)} %fusion.507), custom_call_target="InvertDiagBlocksLowerTriangular" | custom-call | tf_op jit(solution)/shard_map/triangular_solve | solution.py:96
  164.3 2.3 %while.20 = (s32[]{:T(128)}, f32[32,128]{1,0:T(8,128)S(1)}, f32[50]{0:T(128)S(1)}, bf16[49,32,128]{2,1,0:T(8,128)(2,1)S(1)}, s32[]{:T(128)}, /*index=5*/s32[]{:T(128)}, s32[]{:T(128)}, s32[]{:T(128)}, s32[]{:T(128)}) while((s32[]{:T(128)}, f32[32,128]{1,0:T(8,128)S(1)}, f32[50]{0:T(128)S(1)}, bf16[49,32,128]{2,1,0:T(8,128)(2,1)S(1)}, ...), condition=%wide.region_3.4_spmd.clone, body=%wide.region_2.3_spmd.clone.sunk | while | flops 352265 | bytes 237950 | solution.py:150
  167.9 59.0 %all-reduce.10 = (f32[32,128]{1,0:T(8,128)S(1)}, f32[32,128]{1,0:T(8,128)S(1)}) all-reduce(f32[32,128]{1,0:T(8,128)S(1)} %get-tuple-element.164, f32[32,128]{1,0:T(8,128)S(1)} %get-tuple-element.162), channel_id=3, replica_groups=mesh['group'=2,'visit'=16,'sky'=1] {'visit'}, use_global_device_ids=true, to_apply=%region_5.6.clone | all-reduce | flops 8192 | bytes 65536
  (223 shorter events, 58.0 us)
Async XLA Ops:
  0.6 7.2 %copy-start.6 = (bf16[49,31]{0,1:T(8,128)(2,1)S(1)}, bf16[49,31]{0,1:T(8,128)(2,1)}, u32[]{:S(2)}) copy-start(bf16[49,31]{0,1:T(8,128)(2,1)} %param.12) | copy-start | bytes 9118
  0.6 78.4 %collective-permute-start = (bf16[2,128]{1,0:T(2,128)(2,1)}, bf16[2,128]{1,0:T(2,128)(2,1)S(1)}, u32[]{:S(2)}, u32[]{:S(2)}) collective-permute-start(bf16[2,128]{1,0:T(2,128)(2,1)} %param.9), channel_id=1, source_target_pairs={{0,1},{1,0},{2,3},{3,2},{4,5},{5,4},{6,7},{7,6},{8,9},{9,8},{10,11... | collective-permute-start | bytes 1544 | tf_op jit(solution)/shard_map/ppermute | solution.py:113
  4.2 11.1 %copy-start.4 = (s32[1,1,16]{2,1,0:T(1,128)S(1)}, s32[1,1,16]{2,1,0:T(1,128)}, u32[]{:S(2)}) copy-start(s32[1,1,16]{2,1,0:T(1,128)} %param.15) | copy-start | bytes 196
  4.2 11.1 %copy-start.5 = (s32[1,1,16]{2,1,0:T(1,128)S(1)}, s32[1,1,16]{2,1,0:T(1,128)}, u32[]{:S(2)}) copy-start(s32[1,1,16]{2,1,0:T(1,128)} %param.14) | copy-start | bytes 196
  6.0 9.4 %copy-start = (f32[1,32,128]{2,1,0:T(8,128)S(1)}, f32[1,32,128]{2,1,0:T(8,128)}, u32[]{:S(2)}) copy-start(f32[1,32,128]{2,1,0:T(8,128)} %param.11) | copy-start | bytes 49156
  6.0 41.6 %copy-start.1 = (f32[1,32,128]{2,1,0:T(8,128)S(1)}, f32[1,32,128]{2,1,0:T(8,128)}, u32[]{:S(2)}) copy-start(f32[1,32,128]{2,1,0:T(8,128)} %param.10) | copy-start | bytes 49156
  6.0 73.0 %copy-start.3 = (bf16[2,128]{1,0:T(2,128)(2,1)S(1)}, bf16[2,128]{1,0:T(2,128)(2,1)}, u32[]{:S(2)}) copy-start(bf16[2,128]{1,0:T(2,128)(2,1)} %param.9) | copy-start | bytes 1540
  7.8 85.6 %copy-start.7 = (u32[32]{0:T(128)S(1)}, u32[32]{0:T(128)}, u32[]{:S(2)}) copy-start(u32[32]{0:T(128)} %constant.231) | copy-start | bytes 388
  79.1 4.1 %collective-permute-start.1 = (bf16[4,128]{1,0:T(4,128)(2,1)S(1)}, bf16[4,128]{1,0:T(4,128)(2,1)S(1)}, u32[]{:S(2)}, u32[]{:S(2)}) collective-permute-start(bf16[4,128]{1,0:T(4,128)(2,1)S(1)} %maximum_select_fusion.3), channel_id=1, source_target_pairs={{0,2},{1,3},{2,0},{3,1},{4,6},{5,7},{6,4},{7,5},{8,10},{9,11},{10,... | collective-permute-start | bytes 3080 | tf_op jit(solution)/shard_map/ppermute | solution.py:113
  83.2 3.7 %collective-permute-start.2 = (bf16[8,128]{1,0:T(8,128)(2,1)S(1)}, bf16[8,128]{1,0:T(8,128)(2,1)S(1)}, u32[]{:S(2)}, u32[]{:S(2)}) collective-permute-start(bf16[8,128]{1,0:T(8,128)(2,1)S(1)} %maximum_select_fusion.2), channel_id=1, source_target_pairs={{0,4},{1,5},{2,6},{3,7},{4,0},{5,1},{6,2},{7,3},{8,12},{9,13},{10,... | collective-permute-start | bytes 6152 | tf_op jit(solution)/shard_map/ppermute | solution.py:113
  87.0 4.6 %collective-permute-start.3 = (bf16[16,128]{1,0:T(8,128)(2,1)S(1)}, bf16[16,128]{1,0:T(8,128)(2,1)S(1)}, u32[]{:S(2)}, u32[]{:S(2)}) collective-permute-start(bf16[16,128]{1,0:T(8,128)(2,1)S(1)} %maximum_select_fusion.1), channel_id=1, source_target_pairs={{0,8},{1,9},{2,10},{3,11},{4,12},{5,13},{6,14},{7,15},{8,0},{9,1},... | collective-permute-start | bytes 12296 | tf_op jit(solution)/shard_map/ppermute | solution.py:113
  91.7 3.0 %collective-permute-start.4 = (bf16[32,15]{1,0:T(8,128)(2,1)S(1)}, bf16[32,15]{1,0:T(8,128)(2,1)S(1)}, u32[]{:S(2)}, u32[]{:S(2)}) collective-permute-start(bf16[32,15]{1,0:T(8,128)(2,1)S(1)} %get-tuple-element.389), channel_id=1, source_target_pairs={} | collective-permute-start | bytes 2888 | tf_op jit(solution)/shard_map/ppermute | solution.py:18
  92.3 2.4 %collective-permute-start.5 = (bf16[32,15]{1,0:T(8,128)(2,1)S(1)}, bf16[32,15]{1,0:T(8,128)(2,1)S(1)}, u32[]{:S(2)}, u32[]{:S(2)}) collective-permute-start(bf16[32,15]{1,0:T(8,128)(2,1)S(1)} %get-tuple-element.390), channel_id=1, source_target_pairs={} | collective-permute-start | bytes 2888 | tf_op jit(solution)/shard_map/ppermute | solution.py:20
  94.7 4.8 %copy-start.8 = (bf16[7,158,128]{1,0,2:T(8,128)(2,1)S(1)}, bf16[7,158,128]{1,0,2:T(8,128)(2,1)}, u32[]{:S(2)}) copy-start(bf16[7,158,128]{1,0,2:T(8,128)(2,1)} %fusion.28) | copy-start | bytes 849412
  166.6 60.8 %copy-start.2 = (f32[50]{0:T(128)}, f32[50]{0:T(128)S(1)}, u32[]{:S(2)}) copy-start(f32[50]{0:T(128)S(1)} %get-tuple-element.611) | copy-start | bytes 604
